TPU v7x, 256 devices: a whole 4x4x8 slice. The times are simulated.
256 devices in a mesh: slab: 256 (over z, x, y, core).
Axes of the slice: x: 4, y: 4, z: 8, core: 2. Of those that a mesh axis runs over, the one named last changes fastest.
Arguments:
- newton_rhs: float32 [3, 1024, 128, 128], P(None, 'slab'), may hold values from -8 to 8
- stiffness: float32 [1024, 128, 128], P('slab'), may hold values from 0.25 to 4
- stencil: float32 [27, 3, 3], replicated, may hold values from -0.1 to 10.1, as said below
- dual_weight: float32 [1024, 128], P('slab'), may hold values from 0.5 to 2
- mortar: bfloat16 [1024, 3, 128, 128], P('slab'), may hold values from -0.3125 to 0.3125
- partner: int32 [1024, 3], P('slab'), may hold values from 0 to 1023, as said below
- active: int32 [1024], P('slab'), may hold values 0 or 1
Outputs:
- increment: float32 [3, 1024, 128, 128], P(None, 'slab')
- residual: float32 [3, 1024, 128, 128], P(None, 'slab')
Inputs may be any that keep to these rules, and one draw needn't show every extreme that they name: stencil[26 - k] is the transpose of stencil[k]; entries off the centre block lie within 0.1 in magnitude, and the centre block stencil[13] is 10 times the identity plus a symmetric matrix of entries within 0.1. `partner`: slave tile t lies on device d = t // 4; slot s of it names a tile on device (1 - d // 128) * 128 + (d % 128 + s - 1) modulo 128.
All inputs are finite; a program needn't handle non-finite values. No bound on the sum of `active` on one device may be relied on, other than what follows from the above.
Results may differ from a plain program's by a relative error of at most 0.0003.
Values sent between devices are 32-bit elements; how exact they have to be, the bound alone decides.
No kernel may reach another device: no remote copies, remote signals or barrier semaphores. Data moves between devices by JAX's collectives and lax.ppermute only.
A program may use at most 64 MiB of HBM per device.

v0:
```python
import jax
import jax.numpy as jnp
from jax import lax
from jax.sharding import PartitionSpec as P

ITERS = 2


def with_halo(array, sides, width):
    for axis, dim in sides:
        peers, length = (lax.axis_size(axis), array.shape[dim])
        up = [(i, (i + 1) % peers) for i in range(peers)]
        down = [(j, i) for i, j in up]
        last = lax.slice_in_dim(array, length - width, length, axis=dim)
        initial = lax.slice_in_dim(array, 0, width, axis=dim)
        before = lax.ppermute(last, axis, up)
        after = lax.ppermute(initial, axis, down)
        array = jnp.concatenate([before, array, after], axis=dim)
    return array


def stencil_part(field_in, stencil):
    padded = with_halo(field_in, (("slab", 1),), 1)
    slab_index = lax.axis_index("slab")
    quarter_count = lax.axis_size("slab") // 4
    lower_cut = jnp.logical_or(slab_index == quarter_count, slab_index == 3 * quarter_count)
    upper_cut = jnp.logical_or(slab_index == quarter_count - 1, slab_index == 3 * quarter_count - 1)
    lower_rim = jnp.where(lower_cut, 0.0, padded[:, :1])
    upper_rim = jnp.where(upper_cut, 0.0, padded[:, -1:])
    padded = jnp.concatenate([lower_rim, padded[:, 1:-1], upper_rim], axis=1)
    padded = jnp.pad(padded, ((0, 0), (0, 0), (1, 1), (1, 1)))
    plane_count = field_in.shape[1]
    node_count = field_in.shape[2]
    depth_count = field_in.shape[3]
    outputs = [jnp.zeros(field_in.shape[1:], jnp.float32) for out_comp in range(3)]
    for along_x in range(3):
        for along_y in range(3):
            for along_z in range(3):
                offset_index = 9 * along_x + 3 * along_y + along_z
                window_view = padded[
                    :,
                    along_x : along_x + plane_count,
                    along_y : along_y + node_count,
                    along_z : along_z + depth_count,
                ]
                for out_comp in range(3):
                    for in_comp in range(3):
                        outputs[out_comp] = (
                            outputs[out_comp]
                            + stencil[offset_index, out_comp, in_comp] * window_view[in_comp]
                        )
    return jnp.stack(outputs)


def contact_gather(master, slave_face, dual_weight, mortar_full, partner, active_float):
    planes = master.shape[0]
    tile_width = master.shape[1]
    all_faces = lax.all_gather(master, "slab", axis=0, tiled=True)
    facing = jnp.take(all_faces, partner, axis=0)
    pulled = jnp.einsum("tpij,tpj->ti", mortar_full, facing, precision=lax.Precision.HIGHEST)
    push_force = 4.0 * active_float[:, None] * (dual_weight * slave_face - pulled)
    back_force = -jnp.einsum(
        "tpij,ti->tpj", mortar_full, push_force, precision=lax.Precision.HIGHEST
    )
    reaction_table = jnp.zeros((planes * lax.axis_size("slab"), tile_width), jnp.float32)
    reaction_table = reaction_table.at[partner.reshape(-1)].add(back_force.reshape(-1, tile_width))
    master_add = lax.psum_scatter(reaction_table, "slab", scatter_dimension=0, tiled=True)
    return (dual_weight * push_force, master_add)


def apply_operator(field_in, stencil, stiffness, dual_weight, mortar_full, partner, active_float):
    result = stencil_part(field_in, stencil) + stiffness[None] * field_in
    slave_face = field_in[2, :, :, -1]
    master = field_in[2, :, :, 0]
    slave_add, master_add = contact_gather(
        master, slave_face, dual_weight, mortar_full, partner, active_float
    )
    result = result.at[2, :, :, -1].add(slave_add)
    result = result.at[2, :, :, 0].add(master_add)
    return result


def residual_squares(residual):
    return lax.psum(jnp.sum(residual * residual), "slab")


def local(newton_rhs, stiffness, stencil, dual_weight, mortar, partner, active):
    mortar_full = mortar.astype(jnp.float32)
    active_float = active.astype(jnp.float32)
    increment = jnp.zeros_like(newton_rhs)
    residual = newton_rhs
    direction = newton_rhs
    norm_now = residual_squares(residual)
    for iteration in range(ITERS):
        image = apply_operator(
            direction, stencil, stiffness, dual_weight, mortar_full, partner, active_float
        )
        curvature = lax.psum(jnp.sum(direction * image), "slab")
        step_size = norm_now / curvature
        increment = increment + step_size * direction
        residual = residual - step_size * image
        norm_next = residual_squares(residual)
        direction = residual + norm_next / norm_now * direction
        norm_now = norm_next
    return (increment, residual)


def solution(mesh):
    placed = (
        P(None, "slab", None, None),
        P("slab", None, None),
        P(),
        P("slab", None),
        P("slab", None, None, None),
        P("slab", None),
        P("slab"),
    )
    return jax.shard_map(
        local,
        mesh=mesh,
        in_specs=placed,
        out_specs=(P(None, "slab", None, None), P(None, "slab", None, None)),
        check_vma=False,
    )
```

profile of v0, /device:TPU:1, one launch (start us, length us, event | category | flops | bytes accessed | tf_op | source)
XLA Modules:
  0.0 1311.5 jit_solution(6436635839375762363)
XLA Ops:
  7.2 1.1 fusion.25
  8.5 3.3 collective-permute-start.1
  12.7 0.8 reshape.202
  14.1 1.3 slice.2367
  15.4 1.9 fusion.38
  17.3 2.1 fusion.26
  19.4 2.1 fusion.34
  21.5 1.8 fusion.33
  23.3 2.1 fusion.32
  25.4 2.1 fusion.31
  27.5 2.1 fusion.30
  29.6 2.1 fusion.29
  31.6 1.8 fusion.28
  33.5 2.1 fusion.27
  35.6 2.1 fusion.37
  37.7 2.1 fusion.36
  39.8 2.1 fusion.35
  41.8 1.0 slice.2480
  42.8 1.4 copy.57
  44.7 75.9 %all-gather = f32[1,1024,128,1]{2,3,0,1:T(1,128)S(1)} all-gather(f32[1,4,128,1]{2,3,0,1:T(1,128)S(1)} %copy.72), channel_id=2, replica_groups=mesh['slab'=256] {'slab'}, dimensions={1}, use_global_device_ids=true | all-gather | bytes 526336 | tf_op jit(solution)/shard_map/all_gather | solution.py:58
  122.2 2.5 select_maximum_fusion.2
  124.7 59.7 %multiply_add_fusion.7 = (f32[1,4,128,128]{2,1,3,0:T(4,128)S(1)}, f32[1,4,128,128]{2,1,3,0:T(4,128)S(1)}, f32[1,4,128,128]{2,1,3,0:T(4,128)S(1)}, f32[1,4,128,12...) fusion(f32[3,6,130,130]{2,1,3,0:T(8,128)S(1)} %select_maximum_f, ...), kind=kLoop, calls=%fused_computation.50 | loop fusion | flops 10944512 | bytes 22675780 | tf_op jit(solution)/shard_map/add | solution.py:49
  184.4 59.1 %multiply_add_fusion.6 = f32[1,4,128,128]{2,1,3,0:T(4,128)S(1)} fusion(f32[1,4,128,128]{2,1,3,0:T(4,128)S(1)} %get-tuple-element.76, f32[1,4,128,128]{2,1,3,0:T(4,128)S(1)} %get-tuple-element.75, f32[1,4,128,128]{2,1,3,0:T(4,128)S(1)} %get-tuple-element.74, f32[1,4,128,128]{2,1,3,0:T(4,128)S(1)} %get-tuple-element.73, ...), kind=kLoop, calls=%fused_computation.49 | loop fusion | flops 10551296 | bytes 21496132 | tf_op jit(solution)/shard_map/add | solution.py:49
  243.5 59.0 %multiply_add_fusion.5 = f32[1,4,128,128]{2,1,3,0:T(4,128)S(1)} fusion(f32[1,4,128,128]{2,1,3,0:T(4,128)S(1)} %get-tuple-element.76, f32[1,4,128,128]{2,1,3,0:T(4,128)S(1)} %get-tuple-element.75, f32[1,4,128,128]{2,1,3,0:T(4,128)S(1)} %get-tuple-element.74, f32[1,4,128,128]{2,1,3,0:T(4,128)S(1)} %get-tuple-element.73, ...), kind=kLoop, calls=%fused_computation.48 | loop fusion | flops 10551296 | bytes 21496132 | tf_op jit(solution)/shard_map/add | solution.py:49
  303.3 1.4 scatter_custom_fusion
  304.8 0.9 multiply_reduce_fusion.3
  305.6 246.9 %all-reduce.8.cloned.1.call-done = f32[1024,128]{1,0:T(8,128)} async-done(((f32[1024,128]{1,0:T(8,128)}), f32[1024,128]{1,0:T(8,128)}) %all-reduce.8.cloned.1.call-update) | async-done | bytes 524304
  552.5 0.7 fusion.16
  553.2 1.0 multiply_reduce_fusion.2
  554.2 77.8 %all-reduce.4 = (f32[]{:T(128)}, f32[]{:T(128)}) all-reduce(f32[]{:T(128)} %multiply_reduce_fusion.3, f32[]{:T(128)} %multiply_reduce_fusion.2), channel_id=1, replica_groups=mesh['slab'=256] {'slab'}, use_global_device_ids=true, to_apply=%region_1.0 | all-reduce | flops 2 | bytes 16 | tf_op jit(solution)/shard_map/psum | solution.py:84
  633.4 1.0 multiply_reduce_fusion.1
  634.4 73.2 %psum.30 = f32[]{:T(128)} all-reduce(f32[]{:T(128)} %multiply_reduce_fusion.1), channel_id=1, replica_groups=mesh['slab'=256] {'slab'}, use_global_device_ids=true, to_apply=%region_7.9 | all-reduce | flops 1 | bytes 8 | tf_op jit(solution)/shard_map/psum | solution.py:84
  709.1 1.0 fusion.24
  710.2 1.3 collective-permute-start.2
  711.4 72.0 %all-gather.1 = f32[1,1024,128,1]{2,3,0,1:T(1,128)S(1)} all-gather(f32[1,4,128,1]{2,3,0,1:T(1,128)S(1)} %bitcast.335), channel_id=3, replica_groups=mesh['slab'=256] {'slab'}, dimensions={1}, use_global_device_ids=true | all-gather | bytes 526336 | tf_op jit(solution)/shard_map/all_gather | solution.py:58
  784.6 1.1 broadcast_select_fusion.2
  785.9 2.5 select_maximum_fusion
  788.4 59.4 %multiply_add_fusion.4 = (f32[1,4,128,128]{2,1,3,0:T(4,128)S(1)}, f32[1,4,128,128]{2,1,3,0:T(4,128)S(1)}, f32[1,4,128,128]{2,1,3,0:T(4,128)S(1)}, f32[1,4,128,12...) fusion(f32[3,6,130,130]{2,1,3,0:T(8,128)S(1)} %select_maximum_f, ...), kind=kLoop, calls=%fused_computation.43 | loop fusion | flops 10944512 | bytes 22675780 | tf_op jit(solution)/shard_map/add | solution.py:49
  847.9 59.1 %multiply_add_fusion.3 = f32[1,4,128,128]{2,1,3,0:T(4,128)S(1)} fusion(f32[1,4,128,128]{2,1,3,0:T(4,128)S(1)} %get-tuple-element.67, f32[1,4,128,128]{2,1,3,0:T(4,128)S(1)} %get-tuple-element.66, f32[1,4,128,128]{2,1,3,0:T(4,128)S(1)} %get-tuple-element.65, f32[1,4,128,128]{2,1,3,0:T(4,128)S(1)} %get-tuple-element.64, ...), kind=kLoop, calls=%fused_computation.42 | loop fusion | flops 10551296 | bytes 21496132 | tf_op jit(solution)/shard_map/add | solution.py:49
  907.0 59.0 %multiply_add_fusion.2 = f32[1,4,128,128]{2,1,3,0:T(4,128)S(1)} fusion(f32[1,4,128,128]{2,1,3,0:T(4,128)S(1)} %get-tuple-element.67, f32[1,4,128,128]{2,1,3,0:T(4,128)S(1)} %get-tuple-element.66, f32[1,4,128,128]{2,1,3,0:T(4,128)S(1)} %get-tuple-element.65, f32[1,4,128,128]{2,1,3,0:T(4,128)S(1)} %get-tuple-element.64, ...), kind=kLoop, calls=%fused_computation.41 | loop fusion | flops 10551296 | bytes 21496132 | tf_op jit(solution)/shard_map/add | solution.py:49
  966.8 1.5 scatter_custom_fusion.1
  968.3 249.6 %all-reduce.10.cloned.1.call-done = f32[1024,128]{1,0:T(8,128)} async-done(((f32[1024,128]{1,0:T(8,128)}), f32[1024,128]{1,0:T(8,128)}) %all-reduce.10.cloned.1.call-update) | async-done | bytes 524304
  1217.9 0.7 fusion.11
  1218.6 1.0 multiply_reduce_fusion
  1219.6 77.6 %psum.31 = f32[]{:T(128)} all-reduce(f32[]{:T(128)} %multiply_reduce_fusion), channel_id=1, replica_groups=mesh['slab'=256] {'slab'}, use_global_device_ids=true, to_apply=%region_11.13 | all-reduce | flops 1 | bytes 8 | tf_op jit(solution)/shard_map/psum | solution.py:98
  1298.6 1.3 multiply_subtract_fusion
  1299.9 2.3 copy.62
  1302.2 2.3 copy.63
  (59 shorter events, 6.6 us)
Async XLA Ops:
  7.2 114.1 %copy-start = (bf16[4,3,128,128]{3,2,1,0:T(8,128)(2,1)S(1)}, bf16[4,3,128,128]{3,2,1,0:T(8,128)(2,1)}, u32[]{:S(2)}) copy-start(bf16[4,3,128,128]{3,2,1,0:T(8,128)(2,1)} %param.21) | copy-start | bytes 1179652
  7.2 37.1 %copy-start.6 = (s32[4]{0:T(128)S(1)}, s32[4]{0:T(128)}, u32[]{:S(2)}) copy-start(s32[4]{0:T(128)} %param.23) | copy-start | bytes 52
  7.2 37.2 %copy-start.4 = (f32[4,128,128]{2,1,0:T(8,128)S(1)}, f32[4,128,128]{2,1,0:T(8,128)}, u32[]{:S(2)}) copy-start(f32[4,128,128]{2,1,0:T(8,128)} %param.18) | copy-start | bytes 786436
  7.2 545.3 %all-reduce.8.cloned.1.call-start = ((), (), s32[]{:S(2)}) async-start(), calls=%async_computation | async-start | bytes 1048576
  8.5 113.3 %collective-permute-start.1 = (f32[3,1,128,128]{2,1,3,0:T(1,128)S(1)}, f32[3,1,128,128]{2,1,3,0:T(1,128)S(1)}, u32[]{:S(2)}, u32[]{:S(2)}) collective-permute-start(f32[3,1,128,128]{2,1,3,0:T(1,128)S(1)} %copy.46), channel_id=1, source_target_pairs={{1,0},{2,1},{3,2},{4,3},{5,4},{6,5},{7,6},{8,7},{9,8},{10,9},{11,1... | collective-permute-start | bytes 589832 | tf_op jit(solution)/shard_map/ppermute | solution.py:17
  11.9 110.1 %collective-permute-start = (f32[3,1,128,128]{2,1,3,0:T(1,128)S(1)}, f32[3,1,128,128]{2,1,3,0:T(1,128)S(1)}, u32[]{:S(2)}, u32[]{:S(2)}) collective-permute-start(f32[3,1,128,128]{2,1,3,0:T(1,128)S(1)} %copy.45), channel_id=1, source_target_pairs={{0,1},{1,2},{2,3},{3,4},{4,5},{5,6},{6,7},{7,8},{8,9},{9,10},{10,1... | collective-permute-start | bytes 589832 | tf_op jit(solution)/shard_map/ppermute | solution.py:16
  44.5 258.0 %copy-start.2 = (f32[4,128,128]{1,0,2:T(4,128)}, f32[4,128,128]{1,0,2:T(4,128)S(1)}, u32[]{:S(2)}) copy-start(f32[4,128,128]{1,0,2:T(4,128)S(1)} %copy.53) | copy-start | bytes 786436
  121.8 181.5 %copy-start.7 = (s32[12]{0:T(128)}, s32[12]{0:T(128)S(1)}, u32[]{:S(2)}) copy-start(s32[12]{0:T(128)S(1)} %fusion.21) | copy-start | bytes 148
  243.5 59.3 %copy-start.5 = (f32[4,128]{1,0:T(4,128)S(1)}, f32[4,128]{1,0:T(4,128)}, u32[]{:S(2)}) copy-start(f32[4,128]{1,0:T(4,128)} %param.20) | copy-start | bytes 6148
  302.5 2.3 copy-start.1
  304.7 913.2 %all-reduce.10.cloned.1.call-start = ((), (), s32[]{:S(2)}) async-start(), calls=%async_computation.1 | async-start | bytes 1048576
  710.2 74.4 %collective-permute-start.2 = (f32[3,1,128,128]{2,1,3,0:T(1,128)}, f32[3,1,128,128]{2,1,3,0:T(1,128)}, u32[]{:S(2)}, u32[]{:S(2)}) collective-permute-start(f32[3,1,128,128]{2,1,3,0:T(1,128)} %get-tuple-element.79), channel_id=1, source_target_pairs={{0,1},{1,2},{2,3},{3,4},{4,5},{5,6},{6,7},{7,8},{8,9},{9,10},{10,1... | collective-permute-start | bytes 589832 | tf_op jit(solution)/shard_map/ppermute | solution.py:16
  711.4 74.3 %collective-permute-start.3 = (f32[3,1,128,128]{2,1,3,0:T(1,128)}, f32[3,1,128,128]{2,1,3,0:T(1,128)S(1)}, u32[]{:S(2)}, u32[]{:S(2)}) collective-permute-start(f32[3,1,128,128]{2,1,3,0:T(1,128)} %get-tuple-element.80), channel_id=1, source_target_pairs={{1,0},{2,1},{3,2},{4,3},{5,4},{6,5},{7,6},{8,7},{9,8},{10,9},{11,1... | collective-permute-start | bytes 589832 | tf_op jit(solution)/shard_map/ppermute | solution.py:17
  907.0 59.0 %copy-start.3 = (f32[4,128,128]{1,0,2:T(4,128)S(1)}, f32[4,128,128]{1,0,2:T(4,128)}, u32[]{:S(2)}) copy-start(f32[4,128,128]{1,0,2:T(4,128)} %copy-done.2) | copy-start | bytes 786436
Sparse Core Ops, SparseCore 0:
  304.8 247.6 all-reduce.7
  968.4 249.4 all-reduce.9
where the time goes:
time: 1320 us; the launch traced here: 1310 us
  waiting for transfers between devices  497 us (38%)
  blocking collectives  377 us (29%)
  other arithmetic  374 us (28%)
  local copies, waits for them, and re-layouts  39.3 us (3%)
  between operations  18.7 us (1%)
    unnamed x4, waiting for transfers between devices  496 us
    add x6, other arithmetic, stencil_part(): outputs[out_comp]  355 us
    psum x2, blocking collectives, residual_squares(): return lax.psum(jnp.sum(residual * residual), 'slab')  151 us
    all_gather x2, blocking collectives, contact_gather(): all_faces = lax.all_gather(master, 'slab', axis=0, tiled=True)  148 us
    psum x1, blocking collectives, local(): curvature = lax.psum(jnp.sum(direction * image), 'slab')  77.6 us
    slice x14, local copies, waits for them, and re-layouts, stencil_part(): stencil[offset_index, out_comp, in_comp] * window_view[in_comp]  27.6 us
  transfers between devices with their start and end apart: 6, of which 2 were waited for; matrix products, arithmetic and copies ran while one was open for 3% of the time, Pallas kernels for 0%

commit v1 on v0

--- a/solution.py
+++ b/solution.py
@@ -2,6 +2,7 @@
 import jax.numpy as jnp
 from jax import lax
 from jax.sharding import PartitionSpec as P
+from jax.lax import all_to_all, psum
 
 ITERS = 2
 
@@ -55,7 +56,8 @@
 def contact_gather(master, slave_face, dual_weight, mortar_full, partner, active_float):
     planes = master.shape[0]
     tile_width = master.shape[1]
-    all_faces = lax.all_gather(master, "slab", axis=0, tiled=True)
+    current_arr = all_to_all(jnp.stack(psum(1, "slab") * [master], 0), "slab", 0, 0)
+    all_faces = jnp.concatenate(current_arr, 0)
     facing = jnp.take(all_faces, partner, axis=0)
     pulled = jnp.einsum("tpij,tpj->ti", mortar_full, facing, precision=lax.Precision.HIGHEST)
     push_force = 4.0 * active_float[:, None] * (dual_weight * slave_face - pulled)

time: 1320 us -> 1200 us (0.909)
  blocking collectives: 377 us -> 229 us
  starting transfers between devices: 4.7 us -> 35.3 us
  local copies, waits for them, and re-layouts: 39.3 us -> 22.7 us
  waiting for transfers between devices: 497 us -> 511 us
    all_gather x2 -> x0, blocking collectives: 148 us -> none  [contact_gather(): all_faces = lax.all_gather(master, 'slab', axis=0, tiled=True)]
    all_to_all x0 -> x2, starting transfers between devices: none -> 30.6 us  [contact_gather(): all_to_all(jnp.stack(psum(1, 'slab') * [master], 0), 'slab', 0, 0)]
    slice x14, local copies, waits for them, and re-layouts: 27.6 us -> 10 us  [stencil_part(): stencil[offset_index, out_comp, in_comp] * window_view[in_comp]]
    unnamed x4, waiting for transfers between devices: 496 us -> 511 us
  transfers between devices with their start and end apart: 6 -> 8, of which waited for: 2 -> 2; matrix products, arithmetic and copies ran while one was open for 3% -> 32% of each run, Pallas kernels for 0% -> 0%
where the time goes in v1:
time: 1200 us; the launch traced here: 1190 us
  waiting for transfers between devices  511 us (43%)
  other arithmetic  375 us (31%)
  blocking collectives  229 us (19%)
  starting transfers between devices  35.3 us (3%)
  local copies, waits for them, and re-layouts  22.7 us (2%)
  between operations  18.6 us (2%)
    unnamed x4, waiting for transfers between devices  511 us
    add x6, other arithmetic, stencil_part(): outputs[out_comp]  356 us
    psum x2, blocking collectives, residual_squares(): return lax.psum(jnp.sum(residual * residual), 'slab')  151 us
    psum x1, blocking collectives, local(): curvature = lax.psum(jnp.sum(direction * image), 'slab')  77.6 us
    all_to_all x2, starting transfers between devices, contact_gather(): all_to_all(jnp.stack(psum(1, 'slab') * [master], 0), 'slab', 0, 0)  30.6 us
  transfers between devices with their start and end apart: 8, of which 2 were waited for; matrix products, arithmetic and copies ran while one was open for 32% of the time, Pallas kernels for 0%

profile of v1, /device:TPU:1, one launch (start us, length us, event | category | flops | bytes accessed | tf_op | source)
XLA Modules:
  0.0 1193.3 jit_solution(12898774450962638769)
XLA Ops:
  7.2 1.2 fusion.25
  8.5 3.3 collective-permute-start.1
  11.8 0.8 copy.51
  12.6 1.1 slice_reduce_fusion
  13.7 0.9 stack.9
  14.6 17.4 %all-to-all-start = ((f32[256,4,128]{2,1,0:T(4,128)}), f32[256,4,128]{2,1,0:T(4,128)S(1)}, u32[]{:S(2)}, u32[]{:S(2)}) async-start(f32[256,4,128]{2,1,0:T(4,128)} %stack.9), calls=%async_computation | async-start | bytes 1048576 | tf_op jit(solution)/shard_map/all_to_all | solution.py:59
  32.8 0.7 fusion.38
  33.5 0.7 fusion.26
  34.2 0.7 fusion.34
  35.0 0.7 fusion.33
  35.7 0.7 fusion.32
  36.4 0.7 fusion.31
  37.1 0.7 fusion.30
  37.8 0.7 fusion.29
  38.6 0.7 fusion.28
  39.3 0.7 fusion.27
  40.0 0.7 fusion.37
  40.8 0.7 fusion.36
  41.5 0.7 fusion.35
  43.7 1.1 broadcast_select_fusion.3
  44.8 2.5 select_maximum_fusion.2
  47.3 59.9 %multiply_add_fusion.7 = (f32[1,4,128,128]{2,1,3,0:T(4,128)S(1)}, f32[1,4,128,128]{2,1,3,0:T(4,128)S(1)}, f32[1,4,128,128]{2,1,3,0:T(4,128)S(1)}, f32[1,4,128,12...) fusion(f32[3,6,130,130]{2,1,3,0:T(8,128)S(1)} %select_maximum_f, ...), kind=kLoop, calls=%fused_computation.51 | loop fusion | flops 10944512 | bytes 22675780 | tf_op jit(solution)/shard_map/add | solution.py:50
  107.2 59.0 %multiply_add_fusion.6 = f32[1,4,128,128]{2,1,3,0:T(4,128)S(1)} fusion(f32[1,4,128,128]{2,1,3,0:T(4,128)S(1)} %get-tuple-element.74, f32[1,4,128,128]{2,1,3,0:T(4,128)S(1)} %get-tuple-element.73, f32[1,4,128,128]{2,1,3,0:T(4,128)S(1)} %get-tuple-element.72, f32[1,4,128,128]{2,1,3,0:T(4,128)S(1)} %get-tuple-element.71, ...), kind=kLoop, calls=%fused_computation.50 | loop fusion | flops 10551296 | bytes 21496132 | tf_op jit(solution)/shard_map/add | solution.py:50
  166.2 59.1 %multiply_add_fusion.5 = f32[1,4,128,128]{2,1,3,0:T(4,128)S(1)} fusion(f32[1,4,128,128]{2,1,3,0:T(4,128)S(1)} %get-tuple-element.74, f32[1,4,128,128]{2,1,3,0:T(4,128)S(1)} %get-tuple-element.73, f32[1,4,128,128]{2,1,3,0:T(4,128)S(1)} %get-tuple-element.72, f32[1,4,128,128]{2,1,3,0:T(4,128)S(1)} %get-tuple-element.71, ...), kind=kLoop, calls=%fused_computation.49 | loop fusion | flops 10551296 | bytes 21496132 | tf_op jit(solution)/shard_map/add | solution.py:50
  227.3 1.5 scatter_custom_fusion
  228.8 0.9 multiply_reduce_fusion.3
  229.7 255.1 %all-reduce.8.cloned.1.call-done = f32[1024,128]{1,0:T(8,128)} async-done(((f32[1024,128]{1,0:T(8,128)}), f32[1024,128]{1,0:T(8,128)}) %all-reduce.8.cloned.1.call-update) | async-done | bytes 524304
  485.5 1.0 multiply_reduce_fusion.2
  486.5 77.8 %all-reduce.4 = (f32[]{:T(128)}, f32[]{:T(128)}) all-reduce(f32[]{:T(128)} %multiply_reduce_fusion.3, f32[]{:T(128)} %multiply_reduce_fusion.2), channel_id=1, replica_groups=mesh['slab'=256] {'slab'}, use_global_device_ids=true, to_apply=%region_1.0 | all-reduce | flops 2 | bytes 16 | tf_op jit(solution)/shard_map/psum | solution.py:86
  565.7 1.0 multiply_reduce_fusion.1
  566.7 73.3 %psum.30 = f32[]{:T(128)} all-reduce(f32[]{:T(128)} %multiply_reduce_fusion.1), channel_id=1, replica_groups=mesh['slab'=256] {'slab'}, use_global_device_ids=true, to_apply=%region_7.9 | all-reduce | flops 1 | bytes 8 | tf_op jit(solution)/shard_map/psum | solution.py:86
  641.7 1.3 collective-permute-start.2
  643.0 0.9 stack.21
  643.9 13.2 %all-to-all-start.1 = ((f32[256,4,128]{2,1,0:T(4,128)}), f32[256,4,128]{2,1,0:T(4,128)}, u32[]{:S(2)}, u32[]{:S(2)}) async-start(f32[256,4,128]{2,1,0:T(4,128)} %stack.21), calls=%async_computation.1 | async-start | bytes 1048576 | tf_op jit(solution)/shard_map/all_to_all | solution.py:59
  657.5 2.5 select_maximum_fusion
  660.0 59.7 %multiply_add_fusion.4 = (f32[1,4,128,128]{2,1,3,0:T(4,128)S(1)}, f32[1,4,128,128]{2,1,3,0:T(4,128)S(1)}, f32[1,4,128,128]{2,1,3,0:T(4,128)S(1)}, f32[1,4,128,12...) fusion(f32[3,6,130,130]{2,1,3,0:T(8,128)S(1)} %select_maximum_f, ...), kind=kLoop, calls=%fused_computation.43 | loop fusion | flops 10944512 | bytes 22675780 | tf_op jit(solution)/shard_map/add | solution.py:50
  719.7 59.0 %multiply_add_fusion.3 = f32[1,4,128,128]{2,1,3,0:T(4,128)S(1)} fusion(f32[1,4,128,128]{2,1,3,0:T(4,128)S(1)} %get-tuple-element.65, f32[1,4,128,128]{2,1,3,0:T(4,128)S(1)} %get-tuple-element.64, f32[1,4,128,128]{2,1,3,0:T(4,128)S(1)} %get-tuple-element.63, f32[1,4,128,128]{2,1,3,0:T(4,128)S(1)} %get-tuple-element.62, ...), kind=kLoop, calls=%fused_computation.42 | loop fusion | flops 10551296 | bytes 21496132 | tf_op jit(solution)/shard_map/add | solution.py:50
  778.7 59.1 %multiply_add_fusion.2 = f32[1,4,128,128]{2,1,3,0:T(4,128)S(1)} fusion(f32[1,4,128,128]{2,1,3,0:T(4,128)S(1)} %get-tuple-element.65, f32[1,4,128,128]{2,1,3,0:T(4,128)S(1)} %get-tuple-element.64, f32[1,4,128,128]{2,1,3,0:T(4,128)S(1)} %get-tuple-element.63, f32[1,4,128,128]{2,1,3,0:T(4,128)S(1)} %get-tuple-element.62, ...), kind=kLoop, calls=%fused_computation.41 | loop fusion | flops 10551296 | bytes 21496132 | tf_op jit(solution)/shard_map/add | solution.py:50
  838.2 1.6 gather_fusion.1
  841.0 0.8 fusion.15
  842.1 1.5 scatter_custom_fusion.1
  843.7 256.1 %all-reduce.10.cloned.1.call-done = f32[1024,128]{1,0:T(8,128)} async-done(((f32[1024,128]{1,0:T(8,128)}), f32[1024,128]{1,0:T(8,128)}) %all-reduce.10.cloned.1.call-update) | async-done | bytes 524304
  1099.8 0.7 fusion.11
  1100.5 1.0 multiply_reduce_fusion
  1101.5 77.6 %psum.31 = f32[]{:T(128)} all-reduce(f32[]{:T(128)} %multiply_reduce_fusion), channel_id=1, replica_groups=mesh['slab'=256] {'slab'}, use_global_device_ids=true, to_apply=%region_11.13 | all-reduce | flops 1 | bytes 8 | tf_op jit(solution)/shard_map/psum | solution.py:100
  1180.3 1.3 multiply_subtract_fusion
  1181.6 2.3 copy.66
  1183.9 2.3 copy.67
  (68 shorter events, 7.6 us)
Async XLA Ops:
  7.2 219.1 %copy-start = (bf16[4,3,128,128]{3,2,1,0:T(8,128)(2,1)S(1)}, bf16[4,3,128,128]{3,2,1,0:T(8,128)(2,1)}, u32[]{:S(2)}) copy-start(bf16[4,3,128,128]{3,2,1,0:T(8,128)(2,1)} %param.21) | copy-start | bytes 1179652
  7.2 35.1 %copy-start.1 = (f32[3,4,128,128]{3,2,1,0:T(8,128)S(1)}, f32[3,4,128,128]{3,2,1,0:T(8,128)}, u32[]{:S(2)}) copy-start(f32[3,4,128,128]{3,2,1,0:T(8,128)} %param.17) | copy-start | bytes 2359300
  7.2 24.8 %copy-start.6 = (s32[4,3]{1,0:T(4,128)S(1)}, s32[4,3]{1,0:T(4,128)}, u32[]{:S(2)}) copy-start(s32[4,3]{1,0:T(4,128)} %param.22) | copy-start | bytes 148
  7.2 25.0 %copy-start.2 = (f32[27,3,3]{0,2,1:T(4,128)S(1)}, f32[27,3,3]{0,2,1:T(4,128)}, u32[]{:S(2)}) copy-start(f32[27,3,3]{0,2,1:T(4,128)} %param.19) | copy-start | bytes 2920
  7.2 35.4 %copy-start.10 = (s32[4]{0:T(128)S(1)}, s32[4]{0:T(128)}, u32[]{:S(2)}) copy-start(s32[4]{0:T(128)} %param.23) | copy-start | bytes 52
  7.2 35.5 %copy-start.5 = (f32[4,128,128]{2,1,0:T(8,128)S(1)}, f32[4,128,128]{2,1,0:T(8,128)}, u32[]{:S(2)}) copy-start(f32[4,128,128]{2,1,0:T(8,128)} %param.18) | copy-start | bytes 786436
  8.5 35.0 %collective-permute-start.1 = (f32[3,1,128,128]{2,1,3,0:T(1,128)S(1)}, f32[3,1,128,128]{2,1,3,0:T(1,128)S(1)}, u32[]{:S(2)}, u32[]{:S(2)}) collective-permute-start(f32[3,1,128,128]{2,1,3,0:T(1,128)S(1)} %copy.52), channel_id=1, source_target_pairs={{1,0},{2,1},{3,2},{4,3},{5,4},{6,5},{7,6},{8,7},{9,8},{10,9},{11,1... | collective-permute-start | bytes 589832 | tf_op jit(solution)/shard_map/ppermute | solution.py:18
  12.6 31.1 %collective-permute-start = (f32[3,1,128,128]{2,1,3,0:T(1,128)}, f32[3,1,128,128]{2,1,3,0:T(1,128)}, u32[]{:S(2)}, u32[]{:S(2)}) collective-permute-start(f32[3,1,128,128]{2,1,3,0:T(1,128)} %copy.51), channel_id=1, source_target_pairs={{0,1},{1,2},{2,3},{3,4},{4,5},{5,6},{6,7},{7,8},{8,9},{9,10},{10,1... | collective-permute-start | bytes 589832 | tf_op jit(solution)/shard_map/ppermute | solution.py:17
  14.6 211.1 %all-to-all-start = ((f32[256,4,128]{2,1,0:T(4,128)}), f32[256,4,128]{2,1,0:T(4,128)S(1)}, u32[]{:S(2)}, u32[]{:S(2)}) async-start(f32[256,4,128]{2,1,0:T(4,128)} %stack.9), calls=%async_computation | async-start | bytes 1048576 | tf_op jit(solution)/shard_map/all_to_all | solution.py:59
  32.0 452.8 %all-reduce.8.cloned.1.call-start = ((), (), s32[]{:S(2)}) async-start(), calls=%async_computation.2 | async-start | bytes 1048576
  32.1 194.2 %copy-start.8 = (pred[4,3]{1,0:T(4,128)(4,1)}, pred[4,3]{1,0:T(4,128)(4,1)S(1)}, u32[]{:S(2)}) copy-start(pred[4,3]{1,0:T(4,128)(4,1)S(1)} %compare_and_fusion) | copy-start | bytes 40
  42.6 184.2 %copy-start.9 = (f32[4]{0:T(128)}, f32[4]{0:T(128)S(1)}, u32[]{:S(2)}) copy-start(f32[4]{0:T(128)S(1)} %convert_multiply_fusion) | copy-start | bytes 52
  42.9 182.5 %copy-start.3 = (f32[4,128,128]{1,0,2:T(4,128)}, f32[4,128,128]{1,0,2:T(4,128)S(1)}, u32[]{:S(2)}) copy-start(f32[4,128,128]{1,0,2:T(4,128)S(1)} %copy.59) | copy-start | bytes 786436
  166.2 60.6 %copy-start.7 = (f32[4,128]{1,0:T(4,128)S(1)}, f32[4,128]{1,0:T(4,128)}, u32[]{:S(2)}) copy-start(f32[4,128]{1,0:T(4,128)} %param.20) | copy-start | bytes 6148
  641.7 15.4 %collective-permute-start.2 = (f32[3,1,128,128]{2,1,3,0:T(1,128)S(1)}, f32[3,1,128,128]{2,1,3,0:T(1,128)S(1)}, u32[]{:S(2)}, u32[]{:S(2)}) collective-permute-start(f32[3,1,128,128]{2,1,3,0:T(1,128)S(1)} %get-tuple-element.77), channel_id=1, source_target_pairs={{0,1},{1,2},{2,3},{3,4},{4,5},{5,6},{6,7},{7,8},{8,9},{9,10},{10,1... | collective-permute-start | bytes 589832 | tf_op jit(solution)/shard_map/ppermute | solution.py:17
  643.0 14.3 %collective-permute-start.3 = (f32[3,1,128,128]{2,1,3,0:T(1,128)S(1)}, f32[3,1,128,128]{2,1,3,0:T(1,128)S(1)}, u32[]{:S(2)}, u32[]{:S(2)}) collective-permute-start(f32[3,1,128,128]{2,1,3,0:T(1,128)S(1)} %get-tuple-element.78), channel_id=1, source_target_pairs={{1,0},{2,1},{3,2},{4,3},{5,4},{6,5},{7,6},{8,7},{9,8},{10,9},{11,1... | collective-permute-start | bytes 589832 | tf_op jit(solution)/shard_map/ppermute | solution.py:18
  643.9 194.3 %all-to-all-start.1 = ((f32[256,4,128]{2,1,0:T(4,128)}), f32[256,4,128]{2,1,0:T(4,128)}, u32[]{:S(2)}, u32[]{:S(2)}) async-start(f32[256,4,128]{2,1,0:T(4,128)} %stack.21), calls=%async_computation.1 | async-start | bytes 1048576 | tf_op jit(solution)/shard_map/all_to_all | solution.py:59
  657.1 442.7 %all-reduce.10.cloned.1.call-start = ((), (), s32[]{:S(2)}) async-start(), calls=%async_computation.3 | async-start | bytes 1048576
  778.7 59.1 %copy-start.4 = (f32[4,128,128]{1,0,2:T(4,128)S(1)}, f32[4,128,128]{1,0,2:T(4,128)}, u32[]{:S(2)}) copy-start(f32[4,128,128]{1,0,2:T(4,128)} %copy-done.3) | copy-start | bytes 786436
Sparse Core Ops, SparseCore 0:
  228.9 255.8 all-reduce.7
  843.8 255.9 all-reduce.9
